TPU v7x, 512 devices: a whole 4x4x16 slice. The times are simulated.
512 devices in a mesh: line: 16 (over z), bus: 32 (over x, y, core).
Axes of the slice: x: 4, y: 4, z: 16, core: 2. Of those that a mesh axis runs over, the one named last changes fastest.
Arguments:
- transfer_factors: float32 [4096, 65536], P('line', 'bus'), may hold values from -0.24 to 0.24
- line_flows: float32 [4096], P('line'), may hold values from -6 to 6
- from_bus: int32 [4096], replicated, may hold values from 0 to 65535
- to_bus: int32 [4096], replicated, may hold values from 0 to 65535
- tripped: int32 [2, 64], replicated, may hold values from 0 to 4095, as said below
Outputs:
- new_factors: float32 [4096, 65536], P('line', 'bus')
- new_flows: float32 [4096], P('line')
Inputs may be any that keep to these rules, and one draw needn't show every extreme that they name: No line is tripped twice; in every segment at most 8 tripped lines lie in one aligned block of 256 consecutive lines, and some block holds exactly 8.
All inputs are finite; a program needn't handle non-finite values.
Results may differ from a plain program's by a relative error of at most 0.00018.
Values sent between devices are 32-bit elements; how exact they have to be, the bound alone decides.
A program may use at most 64 MiB of HBM per device.

v0:
```python
import jax
import jax.numpy as jnp
from jax import lax
from jax.sharding import PartitionSpec as P

PRECISE = lax.Precision.HIGHEST


def chol_solve(factor_lower, right):
    middle = lax.linalg.triangular_solve(factor_lower, right, left_side=True, lower=True)
    return lax.linalg.triangular_solve(
        factor_lower, middle, left_side=True, lower=True, transpose_a=True
    )


def solve_weights(capacitance, terminal_rows):
    factor_lower = jnp.linalg.cholesky(jnp.dot(capacitance, capacitance.T, precision=PRECISE))
    return chol_solve(factor_lower, jnp.dot(capacitance, terminal_rows.T, precision=PRECISE))


def slot_layout(tripped, local_rows, cap):
    steps, outages = tripped.shape
    block = tripped // local_rows
    earlier = jnp.arange(outages)[None, :] < jnp.arange(outages)[:, None]
    same = (block[:, :, None] == block[:, None, :]) & earlier[None]
    rank = jnp.sum(same, axis=2).astype(jnp.int32)
    seg = jnp.arange(steps, dtype=jnp.int32)[:, None]
    slot = block * (steps * cap) + seg * cap + rank
    return (block, rank, slot)


def per_device(transfer_factors, line_flows, from_bus, to_bus, tripped):
    local_rows, local_cols = transfer_factors.shape
    steps, outages = tripped.shape
    cap = 8
    line_index = lax.axis_index("line")
    bus_index = lax.axis_index("bus")
    ids = tripped.reshape(-1)

    def local_column(bus):
        offset = bus - bus_index * local_cols
        inside = (offset >= 0) & (offset < local_cols)
        values = jnp.take(transfer_factors, jnp.clip(offset, 0, local_cols - 1), axis=1)
        return jnp.where(inside[None, :], values, 0.0)

    terminal_part = local_column(jnp.take(from_bus, ids)) - local_column(jnp.take(to_bus, ids))
    terminal = lax.psum(terminal_part, "bus")
    block, rank, slot = slot_layout(tripped, local_rows, cap)
    mine = (block == line_index)[:, None, :] & (
        rank[:, None, :] == jnp.arange(cap, dtype=jnp.int32)[None, :, None]
    )
    position = jnp.sum(jnp.where(mine, (tripped - line_index * local_rows)[:, None, :], 0), axis=2)
    valid = jnp.any(mine, axis=2).reshape(-1)
    position = position.reshape(-1)
    rows = jnp.where(valid[:, None], jnp.take(transfer_factors, position, axis=0), 0.0)
    small = jnp.concatenate(
        [jnp.take(terminal, position, axis=0), jnp.take(line_flows, position)[:, None]], axis=1
    )
    small = jnp.where(valid[:, None], small, 0.0)
    gathered_rows = lax.all_gather(rows, "line").reshape(-1, local_cols)
    gathered_small = lax.all_gather(small, "line").reshape(-1, small.shape[1])
    slot_flat = slot.reshape(-1)
    outage_rows = jnp.take(gathered_rows, slot_flat, axis=0)
    outage_small = jnp.take(gathered_small, slot_flat, axis=0)
    outage_terms = outage_small[:, : steps * outages]
    outage_flows = outage_small[:, steps * outages]
    identity = jnp.eye(outages, dtype=jnp.float32)
    row_global = line_index * local_rows + jnp.arange(local_rows, dtype=jnp.int32)
    hit = row_global[:, None] == tripped[0][None, :]
    keep1 = 1.0 - jnp.any(hit, axis=1).astype(jnp.float32)
    hit2 = row_global[:, None] == tripped[1][None, :]
    keep12 = keep1 * (1.0 - jnp.any(hit2, axis=1).astype(jnp.float32))
    s1 = slice(0, outages)
    s2 = slice(outages, 2 * outages)
    cap1 = identity - outage_terms[s1, s1]
    rhs1 = jnp.concatenate([terminal[:, s1], outage_terms[s2, s1]], axis=0)
    w1 = solve_weights(cap1, rhs1)
    w1t_local = w1[:, :local_rows].T
    w1t_out2 = w1[:, local_rows:].T
    terminal2 = keep1[:, None] * (
        terminal[:, s2] + jnp.dot(w1t_local, outage_terms[s1, s2], precision=PRECISE)
    )
    out2 = outage_terms[s2, s2] + jnp.dot(w1t_out2, outage_terms[s1, s2], precision=PRECISE)
    cap2 = identity - out2
    w2t = solve_weights(cap2, terminal2).T
    combined = jnp.concatenate([w1t_local + jnp.dot(w2t, w1t_out2, precision=PRECISE), w2t], axis=1)
    factors = keep12[:, None] * (
        transfer_factors + jnp.dot(combined, outage_rows, precision=PRECISE)
    )
    flows = keep12 * (line_flows + jnp.dot(combined, outage_flows, precision=PRECISE))
    return (factors, flows)


def solution(mesh):
    placed = (P("line", "bus"), P("line"), P(), P(), P())
    return jax.shard_map(
        per_device,
        mesh=mesh,
        in_specs=placed,
        out_specs=(P("line", "bus"), P("line")),
        check_vma=False,
    )
```

profile of v0, /device:TPU:6, one launch (start us, length us, event | category | flops | bytes accessed | tf_op | source)
XLA Modules:
  0.0 232.9 jit_solution(3203836839279586236)
XLA Ops:
  8.1 0.8 reshape.325
  8.8 1.1 gather_fusion.5
  10.0 1.6 gather_fusion.7
  11.6 2.9 %copy.28 = f32[256,2048]{0,1:T(8,128)} copy(f32[256,2048]{1,0:T(8,128)} %param.10) | data formatting | bytes 4194304 | tf_op args[0]
  14.6 2.5 %gather_fusion.6 = f32[128,256]{1,0:T(8,128)S(1)} fusion(f32[256,2048]{0,1:T(8,128)} %copy.28, s32[1024]{0:T(1024)S(1)} %get-tuple-element.24), kind=kCustom, calls=%fused_computation.1.clone | custom fusion | bytes 262656 | tf_op jit(solution)/shard_map/jit(_take)/gather | solution.py:43
  17.1 2.3 %gather_fusion.8 = f32[128,256]{1,0:T(8,128)S(1)} fusion(f32[256,2048]{0,1:T(8,128)} %copy.28, s32[1024]{0:T(1024)S(1)} %get-tuple-element.23), kind=kCustom, calls=%fused_computation.3.clone | custom fusion | bytes 262656 | tf_op jit(solution)/shard_map/jit(_take)/gather | solution.py:43
  19.4 0.8 fusion.7
  21.1 0.6 gather_fusion.3
  21.7 0.7 fusion.6
  22.8 0.7 gather_fusion.1
  23.7 133.1 %all-reduce.2.cloned.1.call-done = f32[256,128]{0,1:T(8,128)} async-done(((f32[256,128]{0,1:T(8,128)}), f32[256,128]{0,1:T(8,128)}) %all-reduce.2.cloned.1.call-update) | async-done | bytes 131088 | tf_op jit(solution)/shard_map/psum | solution.py:47
  156.8 1.1 copy.30
  157.9 0.6 gather_fusion
  158.6 31.7 %all_gather.8 = f32[16,16,129]{2,1,0:T(8,128)S(1)} all-gather(f32[1,16,129]{2,1,0:T(8,128)S(1)} %maximum_select_fusion), channel_id=1, replica_groups=mesh['line'=16,'bus'=32] {'line'}, dimensions={0}, use_global_device_ids=true | all-gather | bytes 140352 | tf_op jit(solution)/shard_map/all_gather | solution.py:61
  190.4 0.8 gather_fusion.2
  191.5 5.8 %cholesky.44 = f32[64,64]{1,0:T(8,128)S(1)} custom-call(f32[64,64]{1,0:T(8,128)S(1)} %fusion.25), custom_call_target="Cholesky" | custom-call | tf_op jit(solution)/shard_map/jit(cholesky)/cholesky | solution.py:17
  197.4 0.6 compare_reduce_fusion.3
  198.0 0.7 fusion.14
  198.7 4.9 %custom-call.12 = f32[1,64,64]{1,2,0:T(8,128)S(1)} custom-call(f32[1,64,64]{2,1,0:T(8,128)S(1)} %fusion.14), custom_call_target="InvertDiagBlocksLowerTriangular" | custom-call | tf_op jit(solution)/shard_map/triangular_solve | solution.py:11
  203.7 0.2 fusion.9
  203.9 0.3 fusion.23
  204.2 0.2 fusion.21
  204.4 0.3 fusion.2
  205.0 5.8 %cholesky.55 = f32[64,64]{1,0:T(8,128)S(1)} custom-call(f32[64,64]{1,0:T(8,128)S(1)} %fusion.20), custom_call_target="Cholesky" | custom-call | tf_op jit(solution)/shard_map/jit(cholesky)/cholesky | solution.py:17
  210.9 0.6 compare_reduce_fusion.2
  211.5 0.7 fusion.15
  212.2 4.9 %custom-call.13 = f32[1,64,64]{1,2,0:T(8,128)S(1)} custom-call(f32[1,64,64]{2,1,0:T(8,128)S(1)} %fusion.15), custom_call_target="InvertDiagBlocksLowerTriangular" | custom-call | tf_op jit(solution)/shard_map/triangular_solve | solution.py:11
  217.2 0.3 fusion.1
  217.7 0.3 fusion.18
  218.6 0.6 add_multiply_fusion
  219.2 3.0 %gather_fusion.4 = f32[128,2048]{1,0:T(8,128)S(1)} fusion(f32[256,2048]{1,0:T(8,128)} %bitcast.68, s32[1024]{0:T(1024)S(1)} %pad_clamp_fusion), kind=kCustom, calls=%fused_computation.8 | custom fusion | bytes 2097664 | tf_op jit(solution)/shard_map/jit(_take)/gather | solution.py:63
  222.2 3.3 %fusion = f32[256,2048]{1,0:T(8,128)} fusion(f32[256,2048]{1,0:T(8,128)S(1)} %copy-done.2, f32[128,2048]{1,0:T(8,128)S(1)} %gather_fusion.4, f32[256]{0:T(256)S(1)} %get-tuple-element.16, pred[128]{0:T(512)(128)(4,1)S(1)} %compare_and_fusion.6, f32[256,64]{0,1:T(8,128)S(1)} %bitcast.71, f32[256,64]{0,1:T(8,128)S(1)} %convolution_add_fusion.1), kind=kOutput, calls=%fused_computation.10 | convolution fusion | flops 806649856 | bytes 5375104 | tf_op jit(solution)/shard_map/dot_general | solution.py:88
  (65 shorter events, 3.2 us)
Async XLA Ops:
  8.0 0.8 copy-start
  8.0 148.8 %all-reduce.2.cloned.1.call-start = ((), (), s32[]{:S(2)}) async-start(), calls=%async_computation | async-start | bytes 262144 | tf_op jit(solution)/shard_map/psum | solution.py:47
  14.5 5.8 %copy-start.4 = (s32[2,64]{1,0:T(2,128)S(1)}, s32[2,64]{1,0:T(2,128)}, u32[]{:S(2)}) copy-start(s32[2,64]{1,0:T(2,128)} %param.14) | copy-start | bytes 1540
  14.5 6.6 %copy-start.2 = (f32[256,2048]{1,0:T(8,128)S(1)}, f32[256,2048]{1,0:T(8,128)}, u32[]{:S(2)}) copy-start(f32[256,2048]{1,0:T(8,128)} %param.10) | copy-start | bytes 6291460
  14.6 8.2 %copy-start.1 = (f32[256]{0:T(256)S(1)}, f32[256]{0:T(256)}, u32[]{:S(2)}) copy-start(f32[256]{0:T(256)} %param.11) | copy-start | bytes 3076
  20.2 198.9 %all-gather.2.cloned.1.call-start = ((), (), s32[]{:S(2)}) async-start(), calls=%async_computation.1 | async-start | bytes 2228224 | tf_op jit(solution)/shard_map/all_gather | solution.py:60
  156.8 46.9 %slice-start = ((f32[256,128]{0,1:T(8,128)}), f32[256,64]{0,1:T(8,128)S(1)}, s32[]{:S(2)}) async-start(f32[256,128]{0,1:T(8,128)} %all-reduce.2.cloned.1.call-done), calls=%async_computation.2 | async-start | bytes 131072 | tf_op jit(solution)/shard_map/slice | solution.py:76
  156.8 60.4 %copy-start.3 = (f32[256,128]{0,1:T(8,128)S(1)}, f32[256,128]{0,1:T(8,128)}, u32[]{:S(2)}) copy-start(f32[256,128]{0,1:T(8,128)} %all-reduce.2.cloned.1.call-done) | copy-start | bytes 393220
Sparse Core Ops, SparseCore 0:
  20.4 136.3 all-reduce.1
Sparse Core Ops, SparseCore 1:
  23.4 77.5 all-gather.1
where the time goes:
time: 233 us
  waiting for transfers between devices  133 us (57%)
  blocking collectives  31.7 us (14%)
  other arithmetic  27.3 us (12%)
  local copies, waits for them, and re-layouts  18.9 us (8%)
  between operations  15.8 us (7%)
  matrix products  5.96 us (3%)
    psum x1, waiting for transfers between devices, per_device(): terminal = lax.psum(terminal_part, 'bus')  133 us
    all_gather x1, blocking collectives, per_device(): gathered_small = lax.all_gather(small, 'line').reshape(-1, small.shape[1])  31.7 us
    another operation x6, other arithmetic, solve_weights(): jnp.linalg.cholesky(jnp.dot(capacitance, capacitance.T, precision=PRECISE))  13 us
    another operation x4, other arithmetic, chol_solve(): lax.linalg.triangular_solve(factor_lower, middle, left_side=True, lower=T...  11.1 us
    gather x2, local copies, waits for them, and re-layouts, local_column(): jnp.take(transfer_factors, jnp.clip(offset, 0, local_cols - 1), axis=1)  4.83 us
  transfers between devices with their start and end apart: 2, of which 1 were waited for; matrix products, arithmetic and copies ran while one was open for 14% of the time, Pallas kernels for 0%

commit v1 on v0

--- a/solution.py
+++ b/solution.py
@@ -44,7 +44,7 @@
         return jnp.where(inside[None, :], values, 0.0)
 
     terminal_part = local_column(jnp.take(from_bus, ids)) - local_column(jnp.take(to_bus, ids))
-    terminal = lax.psum(terminal_part, "bus")
+    terminal = jnp.sum(lax.all_gather(terminal_part, "bus"), axis=0)
     block, rank, slot = slot_layout(tripped, local_rows, cap)
     mine = (block == line_index)[:, None, :] & (
         rank[:, None, :] == jnp.arange(cap, dtype=jnp.int32)[None, :, None]

time: 233 us -> 253 us (1.086)
  other arithmetic: 27.3 us -> 40.2 us
  local copies, waits for them, and re-layouts: 18.9 us -> 24.3 us
  matrix products: 5.96 us -> 10.4 us
  waiting for transfers between devices: 133 us -> 130 us
    psum x1 -> x0, waiting for transfers between devices: 133 us -> none  [per_device(): terminal = lax.psum(terminal_part, 'bus')]
    all_gather x1, waiting for transfers between devices: 0.01 us -> 68.9 us  [per_device(): gathered_rows = lax.all_gather(rows, 'line').reshape(-1, local_cols)]
    all_gather x0 -> x1, waiting for transfers between devices: none -> 61.1 us  [per_device(): terminal = jnp.sum(lax.all_gather(terminal_part, 'bus'), axis=0)]
    another operation x4, other arithmetic: 11.1 us -> 15.2 us  [chol_solve(): lax.linalg.triangular_solve(factor_lower, middle, left_side=True, lower=T...]
    gather x2, local copies, waits for them, and re-layouts: 4.83 us -> 1.51 us  [local_column(): jnp.take(transfer_factors, jnp.clip(offset, 0, local_cols - 1), axis=1)]
    unnamed x11 -> x20, local copies, waits for them, and re-layouts: 2.91 us -> 6.09 us
    another operation x6, other arithmetic: 13 us -> 15.9 us  [solve_weights(): jnp.linalg.cholesky(jnp.dot(capacitance, capacitance.T, precision=PRECISE))]
    slice x4 -> x3, local copies, waits for them, and re-layouts: 0.1 us -> 2.93 us  [per_device(): rhs1 = jnp.concatenate([terminal[:, s1], outage_terms[s2, s1]], axis=0)]
  transfers between devices with their start and end apart: 2 -> 2, of which waited for: 1 -> 2; matrix products, arithmetic and copies ran while one was open for 14% -> 5% of each run, Pallas kernels for 0% -> 0%
where the time goes in v1:
time: 253 us; the launch traced here: 251 us
  waiting for transfers between devices  130 us (51%)
  other arithmetic  40.2 us (16%)
  blocking collectives  31.8 us (13%)
  local copies, waits for them, and re-layouts  24.3 us (10%)
  between operations  14.4 us (6%)
  matrix products  10.4 us (4%)
    all_gather x1, waiting for transfers between devices, per_device(): gathered_rows = lax.all_gather(rows, 'line').reshape(-1, local_cols)  68.9 us
    all_gather x1, waiting for transfers between devices, per_device(): terminal = jnp.sum(lax.all_gather(terminal_part, 'bus'), axis=0)  61.1 us
    all_gather x1, blocking collectives, per_device(): gathered_small = lax.all_gather(small, 'line').reshape(-1, small.shape[1])  31.8 us
    another operation x6, other arithmetic, solve_weights(): jnp.linalg.cholesky(jnp.dot(capacitance, capacitance.T, precision=PRECISE))  15.9 us
    another operation x4, other arithmetic, chol_solve(): lax.linalg.triangular_solve(factor_lower, middle, left_side=True, lower=T...  15.2 us
    unnamed x20, local copies, waits for them, and re-layouts  6.09 us
  transfers between devices with their start and end apart: 2, of which 2 were waited for; matrix products, arithmetic and copies ran while one was open for 5% of the time, Pallas kernels for 0%

profile of v1, /device:TPU:6, one launch (start us, length us, event | category | flops | bytes accessed | tf_op | source)
XLA Modules:
  0.0 251.4 jit_solution(13405131121469822929)
XLA Ops:
  9.4 2.2 gather_fusion.3
  13.2 1.9 copy.24
  15.2 1.1 gather_fusion.5
  16.4 1.1 gather_fusion.7
  19.1 0.8 fusion.7
  21.1 68.9 %all-gather.4.cloned.1.call-done = f32[16,16,2048]{2,1,0:T(8,128)} async-done(((f32[1,16,2048]{2,1,0:T(8,128)}), f32[16,16,2048]{2,1,0:T(8,128)}) %all-gather.4.cloned.1.call-update) | async-done | bytes 2097168 | tf_op jit(solution)/shard_map/all_gather | solution.py:60
  90.1 3.0 %gather_fusion.4 = f32[128,2048]{1,0:T(8,128)S(1)} fusion(f32[256,2048]{1,0:T(8,128)} %bitcast.73, s32[1024]{0:T(1024)S(1)} %pad_clamp_fusion), kind=kCustom, calls=%fused_computation.8 | custom fusion | bytes 2097664 | tf_op jit(solution)/shard_map/jit(_take)/gather | solution.py:63
  93.1 61.1 %all-gather.6.cloned.1.call-done = f32[8192,128]{0,1:T(8,128)} async-done(((f32[256,128]{0,1:T(8,128)}), f32[8192,128]{0,1:T(8,128)}) %all-gather.6.cloned.1.call-update) | async-done | bytes 4194320 | tf_op jit(solution)/shard_map/all_gather | solution.py:47
  154.2 3.5 %copy.31 = f32[16,8,32,256]{3,2,1,0:T(8,128)S(1)} copy(f32[16,8,32,256]{3,1,2,0:T(8,128)} %bitcast.75) | data formatting | bytes 8388608
  157.7 1.0 bitcast_reduce_fusion
  159.5 31.8 %all_gather.16 = f32[16,16,129]{2,1,0:T(8,128)S(1)} all-gather(f32[1,16,129]{2,1,0:T(8,128)S(1)} %maximum_select_fusion), channel_id=1, replica_groups=mesh['line'=16,'bus'=32] {'line'}, dimensions={0}, use_global_device_ids=true | all-gather | bytes 140352 | tf_op jit(solution)/shard_map/all_gather | solution.py:61
  191.3 1.4 gather_fusion.2
  192.7 1.0 broadcast_select_fusion
  194.6 0.8 slice.89
  196.2 1.4 fusion.25
  197.6 6.6 %cholesky.44 = f32[64,64]{1,0:T(8,128)S(1)} custom-call(f32[64,64]{1,0:T(8,128)} %fusion.25), custom_call_target="Cholesky" | custom-call | tf_op jit(solution)/shard_map/jit(cholesky)/cholesky | solution.py:17
  204.9 1.3 fusion.14
  206.1 5.7 %custom-call.12 = f32[1,64,64]{1,2,0:T(8,128)S(1)} custom-call(f32[1,64,64]{2,1,0:T(8,128)} %fusion.14), custom_call_target="InvertDiagBlocksLowerTriangular" | custom-call | tf_op jit(solution)/shard_map/triangular_solve | solution.py:11
  211.8 1.5 copy.29
  213.3 1.0 fusion.9
  214.6 1.0 fusion.21
  216.4 0.8 fusion.41
  217.2 1.4 copy.30
  218.7 1.4 fusion.20
  220.1 7.2 %cholesky.55 = f32[64,64]{1,0:T(8,128)} custom-call(f32[64,64]{1,0:T(8,128)} %fusion.20), custom_call_target="Cholesky" | custom-call | tf_op jit(solution)/shard_map/jit(cholesky)/cholesky | solution.py:17
  227.3 0.8 select_reduce_fusion
  228.7 2.0 fusion.15
  230.7 6.3 %custom-call.13 = f32[1,64,64]{1,2,0:T(8,128)} custom-call(f32[1,64,64]{2,1,0:T(8,128)} %fusion.15), custom_call_target="InvertDiagBlocksLowerTriangular" | custom-call | tf_op jit(solution)/shard_map/triangular_solve | solution.py:11
  237.3 0.9 fusion.42
  238.3 1.0 fusion.18
  239.3 1.0 fusion.16
  241.2 3.4 %fusion = f32[256,2048]{1,0:T(8,128)} fusion(f32[256,2048]{1,0:T(8,128)S(1)} %copy-done.3, f32[128,2048]{1,0:T(8,128)S(1)} %gather_fusion.4, f32[256]{0:T(256)S(1)} %get-tuple-element.16, pred[128]{0:T(512)(128)(4,1)S(1)} %compare_and_fusion.6, f32[256,64]{0,1:T(8,128)S(1)} %bitcast.77, f32[256,64]{0,1:T(8,128)S(1)} %convolution_add_fusion.1), kind=kOutput, calls=%fused_computation.11 | convolution fusion | flops 806649856 | bytes 5375104 | tf_op jit(solution)/shard_map/dot_general | solution.py:88
  (74 shorter events, 12.6 us)
Async XLA Ops:
  7.2 8.0 %copy-start = (s32[4096]{0:T(1024)S(1)}, s32[4096]{0:T(1024)}, u32[]{:S(2)}) copy-start(s32[4096]{0:T(1024)} %param.12) | copy-start | bytes 49156
  7.2 82.9 %all-gather.4.cloned.1.call-start = ((), (), s32[]{:S(2)}) async-start(), calls=%async_computation | async-start | bytes 2228224 | tf_op jit(solution)/shard_map/all_gather | solution.py:60
  12.4 141.8 %all-gather.6.cloned.1.call-start = ((), (), s32[]{:S(2)}) async-start(), calls=%async_computation.1 | async-start | bytes 4325376 | tf_op jit(solution)/shard_map/all_gather | solution.py:47
  13.2 3.1 %copy-start.2 = (s32[4096]{0:T(1024)S(1)}, s32[4096]{0:T(1024)}, u32[]{:S(2)}) copy-start(s32[4096]{0:T(1024)} %param.13) | copy-start | bytes 49156
  15.2 5.0 %copy-start.1 = (f32[256]{0:T(256)S(1)}, f32[256]{0:T(256)}, u32[]{:S(2)}) copy-start(f32[256]{0:T(256)} %param.11) | copy-start | bytes 3076
  16.4 4.6 %copy-start.8 = (s32[2,64]{1,0:T(2,128)S(1)}, s32[2,64]{1,0:T(2,128)}, u32[]{:S(2)}) copy-start(s32[2,64]{1,0:T(2,128)} %param.14) | copy-start | bytes 1540
  158.7 32.6 %copy-start.4 = (f32[256,128]{0,1:T(8,128)}, f32[256,128]{0,1:T(8,128)S(1)}, u32[]{:S(2)}) copy-start(f32[256,128]{0,1:T(8,128)S(1)} %bitcast_reduce_fusion) | copy-start | bytes 393220
  191.3 49.9 %copy-start.3 = (f32[256,2048]{1,0:T(8,128)S(1)}, f32[256,2048]{1,0:T(8,128)}, u32[]{:S(2)}) copy-start(f32[256,2048]{1,0:T(8,128)} %param.10) | copy-start | bytes 6291460
  192.7 44.2 %copy-start.5 = (f32[256,128]{0,1:T(8,128)S(1)}, f32[256,128]{0,1:T(8,128)}, u32[]{:S(2)}) copy-start(f32[256,128]{0,1:T(8,128)} %copy-done.4) | copy-start | bytes 393220
  211.8 2.5 copy-start.7
  215.8 0.6 copy-start.6
Sparse Core Ops, SparseCore 0:
  12.5 77.4 all-gather.3
  93.1 61.0 all-gather.5
